TPU v7x, 32 devices: a whole 2x2x4 slice. The times are simulated.
32 devices in a mesh: dp: 8 (over y, x, core), tensor: 4 (over z).
Axes of the slice: x: 2, y: 2, z: 4, core: 2. Of those that a mesh axis runs over, the one named last changes fastest.
Arguments:
- tokens: bfloat16 [16384, 2048], P(('dp', 'tensor')), may hold values from -6 to 6
- segment_ids: int32 [8, 2048], P('dp'), may hold values from 0 to 15, never falling along the last dimension, each value on 1 to 1024 neighbouring positions
- attngain: float32 [2048], replicated, may hold values from 0.5 to 1.5
- attnshift: float32 [2048], replicated, may hold values from -1.75 to 1.75
- queryweight: bfloat16 [2048, 2048], P('dp', 'tensor'), may hold values from -0.125 to 0.125
- querybias: float32 [2048], P('tensor'), may hold values from -3 to 3
- keyvalue: bfloat16 [2048, 256], P('dp'), may hold values from -0.125 to 0.125
- valuebias: float32 [128], replicated, may hold values from -0.3125 to 0.3125
- outweight: bfloat16 [2048, 2048], P('tensor', 'dp'), may hold values from -0.75 to 0.75
- outbias: float32 [2048], replicated, may hold values from -3 to 3
- mlpgain: float32 [2048], replicated, may hold values from 0.5 to 1.5
- mlpshift: float32 [2048], replicated, may hold values from -1.75 to 1.75
- upweight: bfloat16 [2048, 8192], P('dp', 'tensor'), may hold values from -0.125 to 0.125
- upbias: float32 [8192], P('tensor'), may hold values from -3 to 3
- downweight: bfloat16 [8192, 2048], P('tensor', 'dp'), may hold values from -0.0625 to 0.0625
- downbias: float32 [2048], replicated, may hold values from -3 to 3
- cotangent: bfloat16 [16384, 2048], P(('dp', 'tensor')), may hold values from -6 to 6
Outputs:
- layer_output: bfloat16 [16384, 2048], P(('dp', 'tensor'))
- tokens_grad: bfloat16 [16384, 2048], P(('dp', 'tensor'))
- attngain_grad: float32 [2048], replicated
- attnshift_grad: float32 [2048], replicated
- queryweight_grad: float32 [2048, 2048], P('dp', 'tensor')
- querybias_grad: float32 [2048], P('tensor')
- keyvalue_grad: float32 [2048, 256], P('dp')
- valuebias_grad: float32 [128], replicated
- outweight_grad: float32 [2048, 2048], P('tensor', 'dp')
- outbias_grad: float32 [2048], replicated
- mlpgain_grad: float32 [2048], replicated
- mlpshift_grad: float32 [2048], replicated
- upweight_grad: float32 [2048, 8192], P('dp', 'tensor')
- upbias_grad: float32 [8192], P('tensor')
- downweight_grad: float32 [8192, 2048], P('tensor', 'dp')
- downbias_grad: float32 [2048], replicated
Inputs may be any that keep to these rules, and one draw needn't show every extreme that they name: `segment_ids`: along each sequence the document numbers never fall.
All inputs are finite; a program needn't handle non-finite values.
Results may differ from a plain program's by a relative error of at most 0.015.
Values may be sent and summed in bfloat16 or wider, within the bound.
No kernel may reach another device: no remote copies, remote signals or barrier semaphores. Data moves between devices by JAX's collectives and lax.ppermute only.
A program may use at most 256 MiB of HBM per device.

v0:
```python
import jax
import jax.numpy as jnp
from jax import lax
from jax.sharding import PartitionSpec as P

eps_norm = 1e-05


def layer_norm(values, norm_gain, norm_shift):
    row_mean = jnp.mean(values, axis=-1, keepdims=True)
    centered = values - row_mean
    row_var = jnp.mean(centered * centered, axis=-1, keepdims=True)
    return centered * lax.rsqrt(row_var + eps_norm) * norm_gain + norm_shift


def gelu_tanh(values):
    return jax.nn.gelu(values, approximate=True)


def matmul(left_side, right_side):
    return jnp.dot(left_side, right_side, preferred_element_type=jnp.float32)


def matmul_tn(left_side, right_side):
    return lax.dot_general(
        left_side, right_side, (((0,), (0,)), ((), ())), preferred_element_type=jnp.float32
    )


def matmul_nt(left_side, right_side):
    return lax.dot_general(
        left_side, right_side, (((1,), (1,)), ((), ())), preferred_element_type=jnp.float32
    )


def block_scores(query_rows, key_rows, segment, first_row, head_dim):
    block_rows = query_rows.shape[0]
    heads_local = query_rows.shape[1] // head_dim
    length = key_rows.shape[0]
    flat_rows = query_rows.reshape(block_rows * heads_local, head_dim)
    scores = matmul_nt(flat_rows, key_rows).reshape(block_rows, heads_local, length) * head_dim ** (
        -0.5
    )
    positions = first_row + jnp.arange(block_rows, dtype=jnp.int32)
    places = jnp.arange(length, dtype=jnp.int32)
    query_seg = lax.dynamic_slice_in_dim(segment, first_row, block_rows)
    allowed = (query_seg[:, None] == segment[None, :]) & (places[None, :] <= positions[:, None])
    return (jnp.where(allowed[:, None, :], scores, -1e30), flat_rows)


def attend_forward(queries, key_rows, values, segment, head_dim):
    length = key_rows.shape[0]
    block_rows = min(512, length)
    blocks = length // block_rows
    query_width = queries.shape[1]
    heads_local = query_width // head_dim

    def one_block(block_item):
        query_rows, first_row = block_item
        scores, flat_rows = block_scores(query_rows, key_rows, segment, first_row, head_dim)
        totals = jax.nn.logsumexp(scores, axis=-1)
        weights = jnp.exp(scores - totals[:, :, None]).astype(jnp.bfloat16)
        mixed_rows = matmul(weights.reshape(block_rows * heads_local, length), values)
        return (mixed_rows.reshape(block_rows, query_width), totals)

    starts = jnp.arange(blocks, dtype=jnp.int32) * block_rows
    mixed_rows, totals = lax.map(
        one_block, (queries.reshape(blocks, block_rows, query_width), starts)
    )
    return (mixed_rows.reshape(length, query_width), totals)


def attend_backward(queries, key_rows, values, segment, totals, grad_mixed, head_dim):
    length = key_rows.shape[0]
    block_rows = min(512, length)
    blocks = length // block_rows
    query_width = queries.shape[1]
    heads_local = query_width // head_dim

    def one_block(carried, block_item):
        query_rows, grad_rows, block_totals, first_row = block_item
        scores, flat_rows = block_scores(query_rows, key_rows, segment, first_row, head_dim)
        softmax_rows = jnp.exp(scores - block_totals[:, :, None])
        weights = softmax_rows.astype(jnp.bfloat16).reshape(block_rows * heads_local, length)
        grad_flat = grad_rows.reshape(block_rows * heads_local, head_dim)
        grad_probs = matmul_nt(grad_flat, values).reshape(block_rows, heads_local, length)
        row_delta = jnp.sum(softmax_rows * grad_probs, axis=-1, keepdims=True)
        grad_scores = (softmax_rows * (grad_probs - row_delta) * head_dim ** (-0.5)).astype(
            jnp.bfloat16
        )
        grad_scores = grad_scores.reshape(block_rows * heads_local, length)
        grad_query = matmul(grad_scores, key_rows).reshape(block_rows, query_width)
        grad_keys = carried[0] + matmul_tn(grad_scores, flat_rows)
        grad_values = carried[1] + matmul_tn(weights, grad_flat)
        return ((grad_keys, grad_values), grad_query)

    starts = jnp.arange(blocks, dtype=jnp.int32) * block_rows
    zero_grad = jnp.zeros((length, head_dim), jnp.float32)
    (grad_keys, grad_values), grad_query = lax.scan(
        one_block,
        (zero_grad, zero_grad),
        (
            queries.reshape(blocks, block_rows, query_width),
            grad_mixed.reshape(blocks, block_rows, query_width),
            totals,
            starts,
        ),
    )
    return (
        grad_query.reshape(length, query_width),
        jnp.concatenate([grad_keys, grad_values], axis=1),
    )


def on_device(
    tokens,
    segment_ids,
    attngain,
    attnshift,
    queryweight,
    querybias,
    keyvalue,
    valuebias,
    outweight,
    outbias,
    mlpgain,
    mlpshift,
    upweight,
    upbias,
    downweight,
    downbias,
    cotangent,
):
    head_dim = valuebias.shape[0]
    model_width = tokens.shape[1]
    segment = segment_ids[0]
    tensor_index = lax.axis_index("tensor")
    dp_index = lax.axis_index("dp")
    own_rows = tokens.astype(jnp.float32)
    query_full, pair_full, output_full, upper_full, lower_full = (
        lax.all_gather(queryweight, "dp", axis=0, tiled=True),
        lax.all_gather(keyvalue, "dp", axis=0, tiled=True),
        lax.all_gather(outweight, "dp", axis=1, tiled=True),
        lax.all_gather(upweight, "dp", axis=0, tiled=True),
        lax.all_gather(downweight, "dp", axis=1, tiled=True),
    )
    pair_shift = jnp.concatenate([jnp.zeros((head_dim,), jnp.float32), valuebias])
    normed_float, first_pull = jax.vjp(layer_norm, own_rows, attngain, attnshift)
    normed_first = normed_float.astype(jnp.bfloat16)
    normed_all = lax.all_gather(normed_first, "tensor", axis=0, tiled=True)
    pairs_all = (matmul(normed_all, pair_full) + pair_shift).astype(jnp.bfloat16)
    queries = (matmul(normed_all, query_full) + querybias).astype(jnp.bfloat16)
    key_rows = pairs_all[:, :head_dim]
    values = pairs_all[:, head_dim:]
    mixed_float, totals = attend_forward(queries, key_rows, values, segment, head_dim)
    mixed_heads = mixed_float.astype(jnp.bfloat16)
    residual = (
        own_rows
        + lax.psum_scatter(
            matmul(mixed_heads, output_full), "tensor", scatter_dimension=0, tiled=True
        )
        + outbias
    )
    second_float, second_pull = jax.vjp(layer_norm, residual, mlpgain, mlpshift)
    second_all = lax.all_gather(second_float.astype(jnp.bfloat16), "tensor", axis=0, tiled=True)
    preact = matmul(second_all, upper_full) + upbias
    active_float, gelu_pull = jax.vjp(gelu_tanh, preact)
    active = active_float.astype(jnp.bfloat16)
    layer_out = (
        residual
        + lax.psum_scatter(
            matmul(active, lower_full).astype(jnp.bfloat16),
            "tensor",
            scatter_dimension=0,
            tiled=True,
        ).astype(jnp.float32)
        + downbias
    )
    grad_out = cotangent.astype(jnp.float32)
    downbias_part = jnp.sum(grad_out, axis=0)
    grad_all = lax.all_gather(cotangent, "tensor", axis=0, tiled=True)
    grad_active = matmul_nt(grad_all, lower_full)
    grad_pre = gelu_pull(grad_active)[0].astype(jnp.bfloat16)
    upbias_part = jnp.sum(grad_pre.astype(jnp.float32), axis=0)
    upper_local = matmul_tn(second_all, grad_pre)
    lower_local = matmul_tn(active, grad_all)
    upper_grad, lower_grad = (
        lax.psum_scatter(
            upper_local.astype(jnp.bfloat16), "dp", scatter_dimension=0, tiled=True
        ).astype(jnp.float32),
        lax.psum_scatter(
            lower_local.astype(jnp.bfloat16), "dp", scatter_dimension=1, tiled=True
        ).astype(jnp.float32),
    )
    grad_second = lax.psum_scatter(
        matmul_nt(grad_pre, upper_full), "tensor", scatter_dimension=0, tiled=True
    )
    grad_norm_two, second_gain_part, second_shift_part = second_pull(grad_second)
    grad_resid = grad_out + grad_norm_two
    grad_branch = grad_resid.astype(jnp.bfloat16)
    outbias_part = jnp.sum(grad_branch.astype(jnp.float32), axis=0)
    branch_all = lax.all_gather(grad_branch, "tensor", axis=0, tiled=True)
    grad_mixed = matmul_nt(branch_all, output_full).astype(jnp.bfloat16)
    output_local = matmul_tn(mixed_heads, branch_all)
    grad_query, grad_pairs = attend_backward(
        queries, key_rows, values, segment, totals, grad_mixed, head_dim
    )
    grad_queries = grad_query.astype(jnp.bfloat16)
    query_part = jnp.sum(grad_queries.astype(jnp.float32), axis=0)
    query_local = matmul_tn(normed_all, grad_queries)
    query_grad, output_grad = (
        lax.psum_scatter(
            query_local.astype(jnp.bfloat16), "dp", scatter_dimension=0, tiled=True
        ).astype(jnp.float32),
        lax.psum_scatter(
            output_local.astype(jnp.bfloat16), "dp", scatter_dimension=1, tiled=True
        ).astype(jnp.float32),
    )
    combined = lax.psum_scatter(
        jnp.concatenate([matmul_nt(grad_queries, query_full), grad_pairs], axis=1),
        "tensor",
        scatter_dimension=0,
        tiled=True,
    )
    pair_grad = combined[:, model_width:].astype(jnp.bfloat16)
    grad_first = combined[:, :model_width] + matmul_nt(pair_grad, pair_full)
    pair_local = matmul_tn(normed_first, pair_grad)
    value_part = jnp.sum(pair_grad[:, head_dim:].astype(jnp.float32), axis=0)
    grad_norm_one, first_gain_part, first_shift_part = first_pull(grad_first)
    tokens_grad = (grad_resid + grad_norm_one).astype(jnp.bfloat16)
    query_cols = querybias.shape[0]
    upper_cols = upbias.shape[0]
    query_pad = lax.dynamic_update_slice_in_dim(
        jnp.zeros((query_cols * lax.axis_size("tensor"),), jnp.float32),
        query_part,
        tensor_index * query_cols,
        0,
    )
    upper_pad = lax.dynamic_update_slice_in_dim(
        jnp.zeros((upper_cols * lax.axis_size("tensor"),), jnp.float32),
        upbias_part,
        tensor_index * upper_cols,
        0,
    )
    summed = lax.psum(
        (
            first_gain_part,
            first_shift_part,
            second_gain_part,
            second_shift_part,
            outbias_part,
            downbias_part,
            value_part,
            query_pad,
            upper_pad,
            pair_local,
        ),
        ("dp", "tensor"),
    )
    querybias_grad = lax.dynamic_slice_in_dim(summed[7], tensor_index * query_cols, query_cols, 0)
    upbias_grad = lax.dynamic_slice_in_dim(summed[8], tensor_index * upper_cols, upper_cols, 0)
    keyvalue_grad = lax.dynamic_slice_in_dim(
        summed[9], dp_index * keyvalue.shape[0], keyvalue.shape[0], 0
    )
    return (
        layer_out.astype(jnp.bfloat16),
        tokens_grad,
        summed[0],
        summed[1],
        query_grad,
        querybias_grad,
        keyvalue_grad,
        summed[6],
        output_grad,
        summed[4],
        summed[2],
        summed[3],
        upper_grad,
        upbias_grad,
        lower_grad,
        summed[5],
    )


def solution(mesh):
    return jax.shard_map(
        on_device,
        mesh=mesh,
        in_specs=(
            P(("dp", "tensor"), None),
            P("dp", None),
            P(),
            P(),
            P("dp", "tensor"),
            P("tensor"),
            P("dp", None),
            P(),
            P("tensor", "dp"),
            P(),
            P(),
            P(),
            P("dp", "tensor"),
            P("tensor"),
            P("tensor", "dp"),
            P(),
            P(("dp", "tensor"), None),
        ),
        out_specs=(
            P(("dp", "tensor"), None),
            P(("dp", "tensor"), None),
            P(),
            P(),
            P("dp", "tensor"),
            P("tensor"),
            P("dp", None),
            P(),
            P("tensor", "dp"),
            P(),
            P(),
            P(),
            P("dp", "tensor"),
            P("tensor"),
            P("tensor", "dp"),
            P(),
        ),
        check_vma=False,
    )
```

profile of v0, /device:TPU:0, one launch (start us, length us, event | category | flops | bytes accessed | tf_op | source)
XLA Modules:
  0.0 3135.8 jit_solution(4892486609804354791)
XLA Ops:
  36.1 151.8 %all-gather.10.cloned.1.call-done = bf16[2048,2048]{1,0:T(8,128)(2,1)} async-done(((bf16[512,2048]{1,0:T(8,128)(2,1)}), bf16[2048,2048]{1,0:T(8,128)(2,1)}) %all-gather.10.cloned.1.call-update) | async-done | bytes 8388624 | tf_op jit(solution)/shard_map/all_gather | solution.py:150
  194.8 21.2 all-gather.12.cloned.1.call-done
  230.3 236.1 %while.27 = (s32[]{:T(128)}, bf16[4,512,512]{2,1,0:T(8,128)(2,1)}, f32[4,512,4]{1,2,0:T(4,128)}, s32[4]{0:T(128)S(1)}, s32[2048]{0:T(1024)S(1)}, /*index=5*/s32[...) while((s32[]{:T(128)}, bf16[4,512,512]{2,1,0:T(8,128)(2,1)}, ...), condition=%wide.region_5.6_spmd, body=%wide.region_2.5_spmd.sunk | while | flops 2196783616 | bytes 112314584 | solution.py:67
  246.8 20.5 copy.66
  305.8 20.5 copy.66
  423.6 20.5 copy.66
  480.6 279.8 %reduce-scatter.9.cloned.1.call-done = f32[512,2048]{1,0:T(8,128)} async-done(((f32[2048,2048]{1,0:T(8,128)}), f32[512,2048]{1,0:T(8,128)}) %reduce-scatter.9.cloned.1.call-update) | async-done | bytes 4194320 | tf_op jit(solution)/shard_map/reduce_scatter | solution.py:159
  769.5 47.9 %all-gather.20.cloned.1.call-done = bf16[2048,2048]{1,0:T(8,128)(2,1)} async-done(((bf16[256,2048]{1,0:T(8,128)(2,1)}), bf16[2048,2048]{1,0:T(8,128)(2,1)}) %all-gather.20.cloned.1.call-update) | async-done | bytes 8388624 | tf_op jit(solution)/shard_map/all_gather | solution.py:144
  817.5 151.9 %all-gather.18.cloned.1.call-done = bf16[2048,2048]{1,0:T(8,128)(2,1)} async-done(((bf16[512,2048]{1,0:T(8,128)(2,1)}), bf16[2048,2048]{1,0:T(8,128)(2,1)}) %all-gather.18.cloned.1.call-update) | async-done | bytes 8388624 | tf_op jit(solution)/shard_map/all_gather | solution.py:165
  969.3 24.3 fusion.67
  993.6 125.3 %all-gather.24.cloned.1.call-done = bf16[2048,2048]{1,0:T(8,128)(2,1)} async-done(((bf16[512,2048]{1,0:T(8,128)(2,1)}), bf16[2048,2048]{1,0:T(8,128)(2,1)}) %all-gather.24.cloned.1.call-update) | async-done | bytes 8388624 | tf_op jit(solution)/shard_map/all_gather | solution.py:181
  1118.9 56.3 %all-gather.22.cloned.1.call-done = bf16[2048,2048]{1,0:T(8,128)(2,1)} async-done(((bf16[2048,256]{1,0:T(8,128)(2,1)}), bf16[2048,2048]{1,0:T(8,128)(2,1)}) %all-gather.22.cloned.1.call-update) | async-done | bytes 8388624 | tf_op jit(solution)/shard_map/all_gather | solution.py:145
  1175.1 36.0 %convert_reduce_fusion = (f32[2048]{0:T(1024)}, bf16[2048,2048]{1,0:T(8,128)(2,1)}) fusion(f32[2048,2048]{1,0:T(8,128)} %fusion.67, f32[2048]{0:T(1024)S(1)} %copy-done.46, bf16[2048,2048]{1,0:T(8,128)(2,1)} %all-gather.24.cloned.1.call-done, bf16[2048,2048]{1,0:T(8,128)(2,1)} %all-gather.22.cloned.1.call-done), kind=kOutput, calls=%fused_computation.54 | convolution fusion | flops 17276336128 | bytes 41959424 | tf_op jit(solution)/shard_map/dot_general | solution.py:31
  1211.1 24.5 fusion.68
  1235.7 26.5 convolution_convert_fusion.2
  1262.3 253.8 %reduce-scatter.13.cloned.1.call-done = f32[512,2048]{1,0:T(8,128)} async-done(((f32[2048,2048]{1,0:T(8,128)}), f32[512,2048]{1,0:T(8,128)}) %reduce-scatter.13.cloned.1.call-update) | async-done | bytes 4194320 | tf_op jit(solution)/shard_map/reduce_scatter | solution.py:195
  1521.0 142.7 %reduce-scatter.11.cloned.1.call-done = bf16[512,2048]{1,0:T(8,128)(2,1)} async-done(((bf16[2048,2048]{1,0:T(8,128)(2,1)}), bf16[512,2048]{1,0:T(8,128)(2,1)}) %reduce-scatter.11.cloned.1.call-update) | async-done | bytes 2097168 | tf_op jit(solution)/shard_map/reduce_scatter | solution.py:171
  1674.4 150.4 %all-gather.26.cloned.1.call-done = bf16[2048,2048]{1,0:T(8,128)(2,1)} async-done(((bf16[512,2048]{1,0:T(8,128)(2,1)}), bf16[2048,2048]{1,0:T(8,128)(2,1)}) %all-gather.26.cloned.1.call-update) | async-done | bytes 8388624 | tf_op jit(solution)/shard_map/all_gather | solution.py:202
  1836.2 441.3 %while.28 = (s32[]{:T(128)}, f32[2048,128]{1,0:T(8,128)}, f32[2048,128]{1,0:T(8,128)}, bf16[4,512,512]{2,1,0:T(8,128)(2,1)}, s32[4]{0:T(128)S(1)}, /*index=5*/s3...) while((s32[]{:T(128)}, f32[2048,128]{1,0:T(8,128)}, ...), condition=%wide.region_15.16_spmd.clone, body=%wide.region_13.15_spmd.clone.sunk | while | flops 6509564416 | bytes 204523856 | solution.py:99
  1856.8 22.1 multiply_convert_fusion.5
  1966.1 22.1 multiply_convert_fusion.5
  2076.6 22.1 multiply_convert_fusion.5
  2187.1 22.1 multiply_convert_fusion.5
  2292.4 23.8 convolution_convert_fusion.1
  2316.9 27.4 convolution_convert_fusion
  2367.5 237.0 %reduce-scatter.15.cloned.1.call-done = f32[512,2304]{1,0:T(8,128)} async-done(((f32[2048,2304]{1,0:T(8,128)}), f32[512,2304]{1,0:T(8,128)}) %reduce-scatter.15.cloned.1.call-update) | async-done | bytes 4718608 | tf_op jit(solution)/shard_map/reduce_scatter | solution.py:219
  2621.4 59.3 %reduce-scatter.21.cloned.1.call-done = bf16[256,2048]{1,0:T(8,128)(2,1)} async-done(((bf16[2048,2048]{1,0:T(8,128)(2,1)}), bf16[256,2048]{1,0:T(8,128)(2,1)}) %reduce-scatter.21.cloned.1.call-update) | async-done | bytes 1048592 | tf_op jit(solution)/shard_map/reduce_scatter | solution.py:188
  2683.4 71.8 %reduce-scatter.23.cloned.1.call-done = bf16[2048,256]{1,0:T(8,128)(2,1)} async-done(((bf16[2048,2048]{1,0:T(8,128)(2,1)}), bf16[2048,256]{1,0:T(8,128)(2,1)}) %reduce-scatter.23.cloned.1.call-update) | async-done | bytes 1048592 | tf_op jit(solution)/shard_map/reduce_scatter | solution.py:191
  2757.9 42.0 %reduce-scatter.19.cloned.1.call-done = bf16[512,256]{1,0:T(8,128)(2,1)} async-done(((bf16[512,2048]{1,0:T(8,128)(2,1)}), bf16[512,256]{1,0:T(8,128)(2,1)}) %reduce-scatter.19.cloned.1.call-update) | async-done | bytes 262160 | tf_op jit(solution)/shard_map/reduce_scatter | solution.py:215
  2801.7 42.6 %reduce-scatter.17.cloned.1.call-done = bf16[256,512]{1,0:T(8,128)(2,1)} async-done(((bf16[2048,512]{1,0:T(8,128)(2,1)}), bf16[256,512]{1,0:T(8,128)(2,1)}) %reduce-scatter.17.cloned.1.call-update) | async-done | bytes 262160 | tf_op jit(solution)/shard_map/reduce_scatter | solution.py:212
  2846.1 132.1 %all-reduce.7.cloned.1.call-done = (f32[2048]{0:T(1024)}, f32[2048]{0:T(1024)}, f32[2048]{0:T(1024)}, f32[128]{0:T(128)}, f32[2048]{0:T(1024)}, /*index=5*/f32[2...) async-done(((f32[2048]{0:T(1024)}, f32[2048]{0:T(1024)}, f32[2048]{0:T(1024)}, f32[128]{0:T(128)}, f32[2048]{0:T(1024)}, /*index=5*/f32[2048]{0:T(1024)}, ...) | async-done | bytes 90640 | tf_op jit(solution)/shard_map/psum | solution.py:245
  2980.9 137.6 %all-reduce.5.cloned.1.call-done = f32[2048,256]{1,0:T(8,128)} async-done(((f32[2048,256]{1,0:T(8,128)}), f32[2048,256]{1,0:T(8,128)}) %all-reduce.5.cloned.1.call-update) | async-done | bytes 2097168 | tf_op jit(solution)/shard_map/psum | solution.py:245
  (370 shorter events, 688.1 us)
Async XLA Ops:
  7.2 28.9 all-gather.14.cloned.1.call-start
  7.9 180.0 %all-gather.10.cloned.1.call-start = ((), (), s32[]{:S(2)}) async-start(), calls=%async_computation.8 | async-start | bytes 10485760 | tf_op jit(solution)/shard_map/all_gather | solution.py:150
  16.3 199.7 %all-gather.12.cloned.1.call-start = ((), (), s32[]{:S(2)}) async-start(), calls=%async_computation.9 | async-start | bytes 2359296 | tf_op jit(solution)/shard_map/all_gather | solution.py:141
  17.0 449.4 %all-gather.16.cloned.1.call-start = ((), (), s32[]{:S(2)}) async-start(), calls=%async_computation.11 | async-start | bytes 2359296 | tf_op jit(solution)/shard_map/all_gather | solution.py:143
  17.6 742.8 %reduce-scatter.9.cloned.1.call-start = ((), (), s32[]{:S(2)}) async-start(), calls=%async_computation.12 | async-start | bytes 20971520 | tf_op jit(solution)/shard_map/reduce_scatter | solution.py:159
  479.9 280.5 %copy-start.3 = (bf16[512,2048]{1,0:T(8,128)(2,1)S(1)}, bf16[512,2048]{1,0:T(8,128)(2,1)}, u32[]{:S(2)}) copy-start(bf16[512,2048]{1,0:T(8,128)(2,1)} %param.21) | copy-start | bytes 6291460
  479.9 280.5 %copy-start.41 = (f32[2048]{0:T(1024)S(1)}, f32[2048]{0:T(1024)}, u32[]{:S(2)}) copy-start(f32[2048]{0:T(1024)} %param.30) | copy-start | bytes 24580
  479.9 337.5 %all-gather.20.cloned.1.call-start = ((), (), s32[]{:S(2)}) async-start(), calls=%async_computation.14 | async-start | bytes 9437184 | tf_op jit(solution)/shard_map/all_gather | solution.py:144
  480.5 285.4 %copy-start.24 = (f32[2048]{0:T(1024)S(1)}, f32[2048]{0:T(1024)}, u32[]{:S(2)}) copy-start(f32[2048]{0:T(1024)} %param.31) | copy-start | bytes 24580
  480.5 285.4 %copy-start.42 = (f32[2048]{0:T(1024)S(1)}, f32[2048]{0:T(1024)}, u32[]{:S(2)}) copy-start(f32[2048]{0:T(1024)} %param.32) | copy-start | bytes 24580
  480.5 488.8 %all-gather.18.cloned.1.call-start = ((), (), s32[]{:S(2)}) async-start(), calls=%async_computation.13 | async-start | bytes 10485760 | tf_op jit(solution)/shard_map/all_gather | solution.py:165
  768.0 350.9 %all-gather.24.cloned.1.call-start = ((), (), s32[]{:S(2)}) async-start(), calls=%async_computation.17 | async-start | bytes 10485760 | tf_op jit(solution)/shard_map/all_gather | solution.py:181
  768.7 406.4 %all-gather.22.cloned.1.call-start = ((), (), s32[]{:S(2)}) async-start(), calls=%async_computation.15 | async-start | bytes 9437184 | tf_op jit(solution)/shard_map/all_gather | solution.py:145
  769.5 405.7 %copy-start.46 = (f32[2048]{0:T(1024)S(1)}, f32[2048]{0:T(1024)}, u32[]{:S(2)}) copy-start(f32[2048]{0:T(1024)} %param.34) | copy-start | bytes 24580
  769.5 746.7 %reduce-scatter.13.cloned.1.call-start = ((), (), s32[]{:S(2)}) async-start(), calls=%async_computation.18 | async-start | bytes 20971520 | tf_op jit(solution)/shard_map/reduce_scatter | solution.py:195
  1235.7 428.1 %reduce-scatter.11.cloned.1.call-start = ((), (), s32[]{:S(2)}) async-start(), calls=%async_computation.16 | async-start | bytes 10485760 | tf_op jit(solution)/shard_map/reduce_scatter | solution.py:171
  1262.2 253.9 %copy-start.25 = (f32[2048]{0:T(1024)S(1)}, f32[2048]{0:T(1024)}, u32[]{:S(2)}) copy-start(f32[2048]{0:T(1024)} %param.31) | copy-start | bytes 24580
  1262.2 253.9 %copy-start.29 = (f32[512]{0:T(512)S(1)}, f32[512]{0:T(512)}, u32[]{:S(2)}) copy-start(f32[512]{0:T(512)} %copy-done.28) | copy-start | bytes 6148
  1262.2 253.9 %copy-start.33 = (f32[512]{0:T(512)S(1)}, f32[512]{0:T(512)}, u32[]{:S(2)}) copy-start(f32[512]{0:T(512)} %copy-done.32) | copy-start | bytes 6148
  1262.2 258.8 %copy-start.36 = (f32[512]{0:T(512)S(1)}, f32[512]{0:T(512)}, u32[]{:S(2)}) copy-start(f32[512]{0:T(512)} %copy-done.35) | copy-start | bytes 6148
  1262.2 401.5 %copy-start.43 = (f32[2048]{0:T(1024)S(1)}, f32[2048]{0:T(1024)}, u32[]{:S(2)}) copy-start(f32[2048]{0:T(1024)} %param.36) | copy-start | bytes 24580
  1262.3 562.5 %all-gather.26.cloned.1.call-start = ((), (), s32[]{:S(2)}) async-start(), calls=%async_computation.19 | async-start | bytes 10485760 | tf_op jit(solution)/shard_map/all_gather | solution.py:202
  1674.3 930.2 %reduce-scatter.15.cloned.1.call-start = ((), (), s32[]{:S(2)}) async-start(), calls=%async_computation.20 | async-start | bytes 23592960 | tf_op jit(solution)/shard_map/reduce_scatter | solution.py:219
  2292.4 388.3 %reduce-scatter.21.cloned.1.call-start = ((), (), s32[]{:S(2)}) async-start(), calls=%async_computation.24 | async-start | bytes 9437184 | tf_op jit(solution)/shard_map/reduce_scatter | solution.py:188
  2316.2 439.0 %reduce-scatter.23.cloned.1.call-start = ((), (), s32[]{:S(2)}) async-start(), calls=%async_computation.25 | async-start | bytes 9437184 | tf_op jit(solution)/shard_map/reduce_scatter | solution.py:191
  2344.3 455.6 %reduce-scatter.19.cloned.1.call-start = ((), (), s32[]{:S(2)}) async-start(), calls=%async_computation.23 | async-start | bytes 2359296 | tf_op jit(solution)/shard_map/reduce_scatter | solution.py:215
  2354.5 489.9 %reduce-scatter.17.cloned.1.call-start = ((), (), s32[]{:S(2)}) async-start(), calls=%async_computation.21 | async-start | bytes 2359296 | tf_op jit(solution)/shard_map/reduce_scatter | solution.py:212
  2364.3 244.4 %copy-start.4 = (bf16[512,2048]{1,0:T(8,128)(2,1)S(1)}, bf16[512,2048]{1,0:T(8,128)(2,1)}, u32[]{:S(2)}) copy-start(bf16[512,2048]{1,0:T(8,128)(2,1)} %param.21) | copy-start | bytes 6291460
  2364.3 244.4 %copy-start.20 = (bf16[2048,256]{1,0:T(8,128)(2,1)S(1)}, bf16[2048,256]{1,0:T(8,128)(2,1)}, u32[]{:S(2)}) copy-start(bf16[2048,256]{1,0:T(8,128)(2,1)} %all-gather.14.cloned.1.call-done) | copy-start | bytes 3145732
  2364.3 613.9 %all-reduce.7.cloned.1.call-start = ((), (), s32[]{:S(2)}) async-start(), calls=%async_computation.26 | async-start | bytes 181248 | tf_op jit(solution)/shard_map/psum | solution.py:245
  2365.0 245.6 %copy-start.22 = (f32[8192]{0:T(1024)}, f32[8192]{0:T(1024)S(1)}, u32[]{:S(2)}) copy-start(f32[8192]{0:T(1024)S(1)} %dynamic_update_slice.18) | copy-start | bytes 98308
  2617.2 501.3 %all-reduce.5.cloned.1.call-start = ((), (), s32[]{:S(2)}) async-start(), calls=%async_computation.22 | async-start | bytes 4194304 | tf_op jit(solution)/shard_map/psum | solution.py:245
  (50 other events, 1815.0 us)
Sparse Core Ops, SparseCore 0:
  9.9 26.1 all-gather.13
  38.3 149.6 all-gather.9
  189.8 26.1 all-gather.11
  217.7 28.1 all-gather.15
  480.0 280.3 reduce-scatter.8
  762.3 55.1 all-gather.19
  819.7 149.6 all-gather.17
  971.0 147.8 all-gather.23
  1120.9 54.1 all-gather.21
  1235.8 280.3 reduce-scatter.12
  1518.5 145.1 reduce-scatter.10
  1674.4 150.3 all-gather.25
  2292.5 311.9 reduce-scatter.14
  2608.2 72.3 reduce-scatter.20
  2684.0 71.2 reduce-scatter.22
  2758.7 41.1 reduce-scatter.18
  2803.1 41.1 reduce-scatter.16
  2852.9 125.3 all-reduce.6
  2983.6 134.8 all-reduce.4
where the time goes:
time: 3150 us; the launch traced here: 3140 us
  waiting for transfers between devices  2130 us (68%)
  matrix products  474 us (15%)
  local copies, waits for them, and re-layouts  400 us (13%)
  other arithmetic  104 us (3%)
    reduce_scatter x1, waiting for transfers between devices, on_device(): lax.psum_scatter(matmul(mixed_heads, output_full), 'tensor', scatter_dime...  280 us
    psum x2, waiting for transfers between devices, on_device(): lax.psum((first_gain_part, first_shift_part, second_gain_part, second_shi...  270 us
    reduce_scatter x1, waiting for transfers between devices, on_device(): lax.psum_scatter(matmul_nt(grad_pre, upper_full), 'tensor', scatter_dimen...  254 us
    reduce_scatter x1, waiting for transfers between devices, on_device(): lax.psum_scatter(jnp.concatenate([matmul_nt(grad_queries, query_full), gr...  237 us
    all_gather x1, waiting for transfers between devices, on_device(): lax.all_gather(second_float.astype(jnp.bfloat16), 'tensor', axis=0, tiled...  152 us
    all_gather x1, waiting for transfers between devices, on_device(): normed_all = lax.all_gather(normed_first, 'tensor', axis=0, tiled=True)  152 us
    all_gather x1, waiting for transfers between devices, on_device(): branch_all = lax.all_gather(grad_branch, 'tensor', axis=0, tiled=True)  150 us
    reduce_scatter x1, waiting for transfers between devices, on_device(): lax.psum_scatter(matmul(active, lower_full).astype(jnp.bfloat16), 'tensor...  143 us
  transfers between devices with their start and end apart: 19, of which 18 were waited for; matrix products, arithmetic and copies ran while one was open for 13% of the time, Pallas kernels for 0%

commit v1 on v0

v1 whole, which is shorter than its diff:
```python
import functools

import jax
import jax.numpy as jnp
from jax import lax
from jax.experimental import pallas as pl
from jax.experimental.pallas import tpu as pltpu
from jax.sharding import PartitionSpec as P

eps_norm = 1e-05
masked_score = -1e30
bf16 = jnp.bfloat16
f32 = jnp.float32


def dot_nn(left_side, right_side):
    return jnp.dot(left_side, right_side, preferred_element_type=f32)


def dot_tn(left_side, right_side):
    return lax.dot_general(
        left_side, right_side, (((0,), (0,)), ((), ())), preferred_element_type=f32
    )


def dot_nt(left_side, right_side):
    return lax.dot_general(
        left_side, right_side, (((1,), (1,)), ((), ())), preferred_element_type=f32
    )


def norm_stats(values):
    row_mean = jnp.mean(values, axis=-1, keepdims=True)
    centered = values - row_mean
    row_var = jnp.mean(centered * centered, axis=-1, keepdims=True)
    scale = lax.rsqrt(row_var + eps_norm)
    return row_mean, scale


def norm_backward(values, row_mean, scale, gain, grad):
    xhat = (values - row_mean) * scale
    u = grad * gain
    u_mean = jnp.mean(u, axis=-1, keepdims=True)
    ux_mean = jnp.mean(u * xhat, axis=-1, keepdims=True)
    grad_in = (u - u_mean - xhat * ux_mean) * scale
    return grad_in, jnp.sum(grad * xhat, axis=0), jnp.sum(grad, axis=0)


gelu_c = 0.7978845608028654


def gelu_both(v):
    square = v * v
    inner = gelu_c * v * (1.0 + 0.044715 * square)
    t = jnp.tanh(inner)
    half = 0.5 * (1.0 + t)
    value = v * half
    slope = half + 0.5 * v * (1.0 - t * t) * (gelu_c * (1.0 + 3.0 * 0.044715 * square))
    return value, slope


def stack_heads(block, heads, width):
    return jnp.concatenate(
        [block[:, h * width : (h + 1) * width] for h in range(heads)], axis=0
    )


def block_bias(first_key, keys, start_row, query_row):
    key_at = first_key + lax.broadcasted_iota(jnp.int32, (keys, start_row.shape[1]), 0)
    allowed = (key_at >= start_row) & (key_at <= query_row)
    return jnp.where(allowed, 0.0, masked_score)


def attend_forward_kernel(
    heads, width, keys, info_ref, q_ref, kv_ref, start_ref, o_ref, total_ref
):
    at = pl.program_id(1)
    rows = q_ref.shape[0]
    q = stack_heads(q_ref[...], heads, width)
    start_row = start_ref[...]
    query_row = info_ref[2, at] + lax.broadcasted_iota(jnp.int32, (1, rows), 1)
    scale = width**-0.5

    def step(block, carried):
        top, total, mixed = carried
        first_key = pl.multiple_of(block * keys, keys)
        k = kv_ref[pl.ds(first_key, keys), :width]
        v = kv_ref[pl.ds(first_key, keys), width:]
        bias = block_bias(first_key, keys, start_row, query_row)
        scores = dot_nt(k, q) * scale + jnp.concatenate([bias] * heads, axis=1)
        new_top = jnp.maximum(top, jnp.max(scores, axis=0, keepdims=True))
        shrink = jnp.exp(top - new_top)
        part = jnp.exp(scores - new_top)
        total = total * shrink + jnp.sum(part, axis=0, keepdims=True)
        mixed = mixed * shrink + dot_tn(v, part.astype(bf16))
        return new_top, total, mixed

    count = heads * rows
    top, total, mixed = lax.fori_loop(
        info_ref[0, at],
        info_ref[1, at],
        step,
        (
            jnp.full((1, count), masked_score, f32),
            jnp.zeros((1, count), f32),
            jnp.zeros((width, count), f32),
        ),
    )
    out = (mixed / total).T.astype(bf16)
    for h in range(heads):
        o_ref[:, h * width : (h + 1) * width] = out[h * rows : (h + 1) * rows]
    total_ref[...] = (top + jnp.log(total)).reshape(total_ref.shape)


def attend_backward_kernel(
    heads,
    width,
    keys,
    info_ref,
    q_ref,
    grad_ref,
    o_ref,
    kv_ref,
    start_ref,
    total_ref,
    dq_ref,
    dkv_ref,
):
    at = pl.program_id(1)
    rows = q_ref.shape[0]

    @pl.when((pl.program_id(0) == 0) & (at == 0))
    def _():
        dkv_ref[...] = jnp.zeros_like(dkv_ref)

    q = stack_heads(q_ref[...], heads, width)
    grad = stack_heads(grad_ref[...], heads, width)
    out = stack_heads(o_ref[...], heads, width)
    delta = jnp.sum((grad.astype(f32) * out.astype(f32)).T, axis=0, keepdims=True)
    count = heads * rows
    total = total_ref[...].reshape(1, count)
    start_row = start_ref[...]
    query_row = info_ref[2, at] + lax.broadcasted_iota(jnp.int32, (1, rows), 1)
    scale = width**-0.5

    def step(block, dq):
        first_key = pl.multiple_of(block * keys, keys)
        k = kv_ref[pl.ds(first_key, keys), :width]
        v = kv_ref[pl.ds(first_key, keys), width:]
        bias = block_bias(first_key, keys, start_row, query_row)
        scores = dot_nt(k, q) * scale + jnp.concatenate([bias] * heads, axis=1)
        probs = jnp.exp(scores - total)
        dprobs = dot_nt(v, grad)
        dscores = (probs * (dprobs - delta) * scale).astype(bf16)
        dkv_ref[pl.ds(first_key, keys), :width] += dot_nn(dscores, q)
        dkv_ref[pl.ds(first_key, keys), width:] += dot_nn(probs.astype(bf16), grad)
        return dq + dot_tn(k, dscores)

    dq = lax.fori_loop(
        info_ref[0, at], info_ref[1, at], step, jnp.zeros((width, count), f32)
    )
    dq = dq.T.astype(bf16)
    for h in range(heads):
        dq_ref[:, h * width : (h + 1) * width] = dq[h * rows : (h + 1) * rows]


def attend_shapes(qkv, width):
    tokens = qkv.shape[0]
    heads_all = qkv.shape[1] // width - 2
    heads = 4 if heads_all % 4 == 0 else 1
    rows = min(128, tokens)
    return tokens, heads_all, heads, heads_all // heads, rows, tokens // rows


def attend_forward(qkv, kv_all, info, starts, width, keys):
    tokens, heads_all, heads, groups, rows, blocks = attend_shapes(qkv, width)
    return pl.pallas_call(
        functools.partial(attend_forward_kernel, heads, width, keys),
        grid_spec=pltpu.PrefetchScalarGridSpec(
            num_scalar_prefetch=1,
            grid=(groups, blocks),
            in_specs=[
                pl.BlockSpec((rows, heads * width), lambda g, i, info: (i, g)),
                pl.BlockSpec(kv_all.shape, lambda g, i, info: (0, 0)),
                pl.BlockSpec((1, rows), lambda g, i, info: (0, i)),
            ],
            out_specs=[
                pl.BlockSpec((rows, heads * width), lambda g, i, info: (i, g)),
                pl.BlockSpec((1, 1, 1, heads * rows), lambda g, i, info: (g, i, 0, 0)),
            ],
        ),
        out_shape=[
            jax.ShapeDtypeStruct((tokens, heads_all * width), bf16),
            jax.ShapeDtypeStruct((groups, blocks, 1, heads * rows), f32),
        ],
        name="attend_forward",
    )(info, qkv, kv_all, starts)


def attend_backward(qkv, grad, mixed, kv_all, info, starts, totals, width, keys):
    tokens, heads_all, heads, groups, rows, blocks = attend_shapes(qkv, width)
    tile = pl.BlockSpec((rows, heads * width), lambda g, i, info: (i, g))
    return pl.pallas_call(
        functools.partial(attend_backward_kernel, heads, width, keys),
        grid_spec=pltpu.PrefetchScalarGridSpec(
            num_scalar_prefetch=1,
            grid=(groups, blocks),
            in_specs=[
                tile,
                tile,
                tile,
                pl.BlockSpec(kv_all.shape, lambda g, i, info: (0, 0)),
                pl.BlockSpec((1, rows), lambda g, i, info: (0, i)),
                pl.BlockSpec((1, 1, 1, heads * rows), lambda g, i, info: (g, i, 0, 0)),
            ],
            out_specs=[
                tile,
                pl.BlockSpec(kv_all.shape, lambda g, i, info: (0, 0)),
            ],
        ),
        out_shape=[
            jax.ShapeDtypeStruct((tokens, heads_all * width), bf16),
            jax.ShapeDtypeStruct(kv_all.shape, f32),
        ],
        name="attend_backward",
    )(info, qkv, grad, mixed, kv_all, starts, totals)


class Ring:
    def __init__(self, size):
        self.size = size
        self.chips = size // 2
        half = self.chips // 2
        if half:
            self.order = list(range(half)) + list(range(self.chips - 1, half - 1, -1))
        else:
            self.order = [0]
        n = self.chips
        self.right = [
            (2 * self.order[i] + k, 2 * self.order[(i + 1) % n] + k)
            for i in range(n)
            for k in (0, 1)
        ]
        self.left = [(b, a) for a, b in self.right]
        self.swap = [(i, i ^ 1) for i in range(size)]
        self.far = n // 2
        offsets = [0]
        for s in range(1, self.far):
            offsets += [s, -s]
        if self.far:
            offsets.append(self.far)
        self.offsets = offsets

    def owner(self, index, offset, other):
        place = [0] * self.chips
        for i, chip in enumerate(self.order):
            place[chip] = i
        chip = index // 2
        core = index % 2
        at = jnp.array(place, jnp.int32)[chip]
        there = jnp.array(self.order, jnp.int32)[(at + offset) % self.chips]
        return 2 * there + (1 - core if other else core)

    def send(self, value, pairs):
        return lax.ppermute(value, "dp", pairs)

    def gather(self, own):
        rows = own.shape[0]
        cut = rows // 2
        found = {0: own}
        from_left = from_right = own
        for s in range(1, self.far):
            from_left = self.send(from_left, self.right)
            from_right = self.send(from_right, self.left)
            found[-s] = from_left
            found[s] = from_right
        if self.far:
            low = self.send(from_left[:cut], self.right)
            high = self.send(from_right[cut:], self.left)
            found[self.far] = jnp.concatenate([low, high], axis=0)
        blocks = {}
        for offset in self.offsets:
            blocks[(offset, 0)] = found[offset]
            blocks[(offset, 1)] = self.send(found[offset], self.swap)
        return blocks

    def scatter_sum(self, part):
        summed = {}
        for offset in reversed(self.offsets):
            there = self.send(part(offset, 1).astype(bf16), self.swap)
            summed[offset] = part(offset, 0) + there.astype(f32)
        if not self.far:
            return summed[0]
        cut = summed[0].shape[0] // 2
        result = summed[0]
        for sign, pairs in ((1, self.right), (-1, self.left)):
            held = None
            for s in range(self.far, 0, -1):
                if s == self.far:
                    message = summed[s][:cut] if sign > 0 else summed[s][cut:]
                elif s == self.far - 1:
                    message = self.add_half(summed[sign * s], held, sign, cut)
                else:
                    message = summed[sign * s] + held
                held = self.send(message.astype(bf16), pairs).astype(f32)
            if self.far == 1:
                result = self.add_half(result, held, sign, cut)
            else:
                result = result + held
        return result

    def add_half(self, value, held, sign, cut):
        if sign > 0:
            return jnp.concatenate([value[:cut] + held, value[cut:]], axis=0)
        return jnp.concatenate([value[:cut], value[cut:] + held], axis=0)


def on_device(
    tokens,
    segment_ids,
    attngain,
    attnshift,
    queryweight,
    querybias,
    keyvalue,
    valuebias,
    outweight,
    outbias,
    mlpgain,
    mlpshift,
    upweight,
    upbias,
    downweight,
    downbias,
    cotangent,
):
    head_dim = valuebias.shape[0]
    count, model = tokens.shape
    n_dp = lax.axis_size("dp")
    n_tensor = lax.axis_size("tensor")
    dp_index = lax.axis_index("dp")
    tensor_index = lax.axis_index("tensor")
    ring = Ring(n_dp)
    order = [(o, c) for o in ring.offsets for c in (0, 1)]
    segment = segment_ids[0]
    length = segment.shape[0]
    rows = tokens.astype(f32)
    depth = queryweight.shape[0]
    width = queryweight.shape[1]

    out_turned = outweight.T
    both = lax.all_gather(jnp.stack([queryweight, out_turned]), "tensor", axis=0)
    query_rows = both[:, 0].transpose(1, 0, 2).reshape(depth, n_tensor * width)
    out_rows = both[:, 1].transpose(1, 0, 2).reshape(depth, n_tensor * width)
    first_rows = jnp.concatenate([query_rows, keyvalue], axis=1)

    def whole(block):
        parts = ring.gather(block)
        full = jnp.zeros((n_dp * block.shape[0], block.shape[1]), block.dtype)
        for key in order:
            at = ring.owner(dp_index, *key) * block.shape[0]
            full = lax.dynamic_update_slice_in_dim(full, parts[key], at, 0)
        return full

    first_full = whole(first_rows)
    out_full = whole(out_rows)

    hidden_own = upweight.shape[1] // n_dp

    def hidden_slice(turned):
        mine = lax.all_to_all(turned, "dp", 0, 1, tiled=True)
        return lax.all_gather(mine, "tensor", axis=0, tiled=True)

    up_turned = hidden_slice(upweight.T)
    down_full = hidden_slice(downweight)
    bias_part = lax.dynamic_slice_in_dim(upbias, dp_index * hidden_own, hidden_own)
    biases = lax.all_gather(jnp.concatenate([querybias, bias_part]), "tensor", axis=0)
    query_shift = biases[:, :width].reshape(-1)
    up_shift = biases[:, width:].reshape(-1)

    first_mean, first_scale = norm_stats(rows)
    normed_first = ((rows - first_mean) * first_scale * attngain + attnshift).astype(bf16)
    shift = jnp.concatenate([query_shift, jnp.zeros((head_dim,), f32), valuebias])
    qkv = (dot_nn(normed_first, first_full) + shift).astype(bf16)
    kv_all = lax.all_gather(qkv[:, model:], "tensor", axis=0, tiled=True)

    keys = 256 if length % 256 == 0 else 128
    query_block = min(128, count)
    first_row = tensor_index * count
    own_segment = lax.dynamic_slice_in_dim(segment, first_row, count)
    starts = jnp.sum(
        (segment[None, :] < own_segment[:, None]).astype(jnp.int32), axis=1
    )
    block_first = first_row + jnp.arange(count // query_block, dtype=jnp.int32) * query_block
    info = jnp.stack(
        [
            starts[::query_block] // keys,
            (block_first + query_block - 1) // keys + 1,
            block_first,
        ]
    ).astype(jnp.int32)
    starts = starts.reshape(1, count)
    mixed, totals = attend_forward(qkv, kv_all, info, starts, head_dim, keys)
    residual = rows + dot_nt(mixed, out_full) + outbias
    second_mean, second_scale = norm_stats(residual)
    normed_second = ((residual - second_mean) * second_scale * mlpgain + mlpshift).astype(bf16)

    grads = ring.gather(cotangent)
    seconds = ring.gather(normed_second)
    active, grad_pre = {}, {}
    for key in order:
        preact = dot_nt(seconds[key], up_turned) + up_shift
        value, slope = gelu_both(preact)
        active[key] = value.astype(bf16)
        grad_pre[key] = (dot_nt(grads[key], down_full) * slope).astype(bf16)
    grad_second = ring.scatter_sum(lambda o, c: dot_nn(grad_pre[(o, c)], up_turned))
    second_out = ring.scatter_sum(lambda o, c: dot_nn(active[(o, c)], down_full))
    layer_out = residual + second_out + downbias

    def joined(parts):
        return jnp.concatenate([parts[key] for key in order], axis=0)

    pre_all = joined(grad_pre)
    upbias_part = jnp.sum(pre_all.astype(f32), axis=0)
    up_local = dot_tn(pre_all, joined(seconds))
    down_local = dot_tn(joined(active), joined(grads))

    def hidden_owner(local):
        part = lax.psum_scatter(local.astype(bf16), "tensor", scatter_dimension=0, tiled=True)
        return lax.all_to_all(part, "dp", 1, 0, tiled=True).astype(f32)

    down_grad = hidden_owner(down_local)
    up_grad = hidden_owner(up_local).T

    grad_out = cotangent.astype(f32)
    grad_two, mlpgain_part, mlpshift_part = norm_backward(
        residual, second_mean, second_scale, mlpgain, grad_second
    )
    grad_resid = grad_out + grad_two
    grad_branch = grad_resid.astype(bf16)
    grad_mixed = dot_nn(grad_branch, out_full).astype(bf16)
    grad_queries, grad_kv = attend_backward(
        qkv, grad_mixed, mixed, kv_all, info, starts, totals, head_dim, keys
    )
    grad_pairs = lax.psum_scatter(grad_kv, "tensor", scatter_dimension=0, tiled=True).astype(bf16)
    grad_qkv = jnp.concatenate([grad_queries, grad_pairs], axis=1)
    grad_first = dot_nt(grad_qkv, first_full)
    grad_one, attngain_part, attnshift_part = norm_backward(
        rows, first_mean, first_scale, attngain, grad_first
    )
    tokens_grad = (grad_resid + grad_one).astype(bf16)

    def depth_owner(local):
        def part(offset, other):
            at = ring.owner(dp_index, offset, other) * depth
            return lax.dynamic_slice_in_dim(local, at, depth, 0)

        return ring.scatter_sum(part)

    def width_owner(block):
        parts = block.astype(bf16).reshape(depth, n_tensor, width).transpose(1, 0, 2)
        return lax.psum_scatter(parts, "tensor", scatter_dimension=0, tiled=False).astype(f32)

    out_grad = width_owner(depth_owner(dot_tn(grad_branch, mixed))).T
    first_part = depth_owner(dot_tn(normed_first, grad_qkv))
    query_grad = width_owner(first_part[:, :model])
    pair_part = lax.all_gather(first_part[:, model:], "tensor", axis=0)
    keyvalue_grad = jnp.sum(pair_part, axis=0)

    shift_part = jnp.sum(grad_qkv.astype(f32), axis=0)
    vectors = [
        attngain_part,
        attnshift_part,
        mlpgain_part,
        mlpshift_part,
        jnp.sum(grad_branch.astype(f32), axis=0),
        jnp.sum(grad_out, axis=0),
        shift_part[:model],
        shift_part[model + head_dim :],
        upbias_part,
    ]
    sizes = [v.shape[0] for v in vectors]
    over_tensor = jnp.sum(lax.all_gather(jnp.concatenate(vectors), "tensor", axis=0), axis=0)
    plain = sum(sizes[:-1])
    up_own = lax.dynamic_slice_in_dim(
        over_tensor, plain + tensor_index * hidden_own, hidden_own
    )
    gathered = lax.all_gather(
        jnp.concatenate([over_tensor[:plain], up_own]), "dp", axis=0
    )
    summed = jnp.sum(gathered[:, :plain], axis=0)
    upbias_grad = gathered[:, plain:].reshape(-1)
    found = []
    at = 0
    for size in sizes[:-1]:
        found.append(summed[at : at + size])
        at += size
    querybias_grad = lax.dynamic_slice_in_dim(found[6], tensor_index * width, width)
    return (
        layer_out.astype(bf16),
        tokens_grad,
        found[0],
        found[1],
        query_grad,
        querybias_grad,
        keyvalue_grad,
        found[7],
        out_grad,
        found[4],
        found[2],
        found[3],
        up_grad,
        upbias_grad,
        down_grad,
        found[5],
    )


def solution(mesh):
    return jax.shard_map(
        on_device,
        mesh=mesh,
        in_specs=(
            P(("dp", "tensor"), None),
            P("dp", None),
            P(),
            P(),
            P("dp", "tensor"),
            P("tensor"),
            P("dp", None),
            P(),
            P("tensor", "dp"),
            P(),
            P(),
            P(),
            P("dp", "tensor"),
            P("tensor"),
            P("tensor", "dp"),
            P(),
            P(("dp", "tensor"), None),
        ),
        out_specs=(
            P(("dp", "tensor"), None),
            P(("dp", "tensor"), None),
            P(),
            P(),
            P("dp", "tensor"),
            P("tensor"),
            P("dp", None),
            P(),
            P("tensor", "dp"),
            P(),
            P(),
            P(),
            P("dp", "tensor"),
            P("tensor"),
            P("tensor", "dp"),
            P(),
        ),
        check_vma=False,
    )
```

time: 3150 us -> 1130 us (0.36)
  waiting for transfers between devices: 2130 us -> 484 us
  local copies, waits for them, and re-layouts: 400 us -> 137 us
  matrix products: 474 us -> 248 us
  blocking collectives: 0 us -> 58.9 us
  starting transfers between devices: 0.77 us -> 55.5 us
  Pallas kernels: 0 us -> 39.1 us
  other arithmetic: 104 us -> 72.4 us
    reduce_scatter x8 -> x5, waiting for transfers between devices: 1130 us -> 149 us  [the longest x2 134 us: hidden_owner(): lax.psum_scatter(local.astype(bf16), 'tensor', scatter_dimension=0, tiled...]
    all_gather x9 -> x5, waiting for transfers between devices: 723 us -> 25.3 us  [the longest x1 25.3 us: on_device(): lax.all_gather(jnp.stack([queryweight, out_turned]), 'tensor', axis=0)]
    ppermute x0 -> x64, waiting for transfers between devices: none -> 293 us  [send(): return lax.ppermute(value, 'dp', pairs)]
    psum x2 -> x0, waiting for transfers between devices: 270 us -> none  [on_device(): lax.psum((first_gain_part, first_shift_part, second_gain_part, second_shi...]
    convert_element_type x12 -> x2, local copies, waits for them, and re-layouts: 180 us -> 4.46 us  [scatter_sum(): there = self.send(part(offset, 1).astype(bf16), self.swap)]
    reshape x20 -> x1, local copies, waits for them, and re-layouts: 153 us -> 1.06 us  [width_owner(): block.astype(bf16).reshape(depth, n_tensor, width).transpose(1, 0, 2)]
    dot_general x39 -> x40, matrix products: 385 us -> 248 us  [the longest x18 104 us: dot_nt(): lax.dot_general(left_side, right_side, (((1,), (1,)), ((), ())), preferre...]
    sub x4 -> x0, matrix products: 88.3 us -> none  [one_block(): grad_probs - row_delta]
  transfers between devices with their start and end apart: 19 -> 77, of which waited for: 18 -> 25; matrix products, arithmetic and copies ran while one was open for 13% -> 36% of each run, Pallas kernels for 0% -> 2%
where the time goes in v1:
time: 1130 us; the launch traced here: 1120 us
  waiting for transfers between devices  484 us (43%)
  matrix products  248 us (22%)
  local copies, waits for them, and re-layouts  137 us (12%)
  other arithmetic  72.4 us (6%)
  blocking collectives  58.9 us (5%)
  starting transfers between devices  55.5 us (5%)
  Pallas kernels  39.1 us (3%)
  between operations  22.7 us (2%)
    ppermute x64, waiting for transfers between devices, send(): return lax.ppermute(value, 'dp', pairs)  293 us
    reduce_scatter x2, waiting for transfers between devices, hidden_owner(): lax.psum_scatter(local.astype(bf16), 'tensor', scatter_dimension=0, tiled...  134 us
    dot_general x18, matrix products, dot_nt(): lax.dot_general(left_side, right_side, (((1,), (1,)), ((), ())), preferre...  104 us
    dot_general x18, matrix products, dot_nn(): return jnp.dot(left_side, right_side, preferred_element_type=f32)  83.2 us
    dot_general x4, matrix products, dot_tn(): lax.dot_general(left_side, right_side, (((0,), (0,)), ((), ())), preferre...  60.9 us
    unnamed x183, local copies, waits for them, and re-layouts  57 us
    ppermute x64, starting transfers between devices, send(): return lax.ppermute(value, 'dp', pairs)  42.8 us
    all_gather x1, waiting for transfers between devices, on_device(): lax.all_gather(jnp.stack([queryweight, out_turned]), 'tensor', axis=0)  25.3 us
  transfers between devices with their start and end apart: 77, of which 25 were waited for; matrix products, arithmetic and copies ran while one was open for 36% of the time, Pallas kernels for 2%

profile of v1, /device:TPU:0, one launch (start us, length us, event | category | flops | bytes accessed | tf_op | source)
XLA Modules:
  0.0 1117.4 jit_solution(15521811368037527452)
XLA Ops:
  18.9 15.0 %all-gather.5 = f32[4,1,768]{2,1,0:T(1,128)S(1)} all-gather(f32[1,1,768]{2,1,0:T(1,128)S(1)} %reshape.314), channel_id=3, replica_groups=mesh['dp'=8,'tensor'=4] {'tensor'}, dimensions={0}, use_global_device_ids=true | all-gather | bytes 15360 | tf_op jit(solution)/shard_map/all_gather | solution.py:377
  34.0 25.3 %all-gather.20.cloned.1.call-done = bf16[8,256,512]{2,1,0:T(8,128)(2,1)} async-done(((bf16[2,256,512]{2,1,0:T(8,128)(2,1)}), bf16[8,256,512]{2,1,0:T(8,128)(2,1)}) %all-gather.20.cloned.1.call-update) | async-done | bytes 2097168 | tf_op jit(solution)/shard_map/all_gather | solution.py:352
  72.1 24.8 %collective-permute-done.1 = bf16[256,2304]{0,1:T(8,128)(2,1)} collective-permute-done((bf16[256,2304]{0,1:T(8,128)(2,1)}, bf16[256,2304]{0,1:T(8,128)(2,1)}, u32[]{:S(2)}, u32[]{:S(2)}) %collective-permute-start.1) | collective-permute-done | bytes 1179680 | tf_op jit(solution)/shard_map/ppermute | solution.py:265
  105.6 8.5 collective-permute-done.5
  120.2 9.5 fusion.6.q_ref
  133.2 18.8 %all_to_all.64 = bf16[8,256,256]{2,1,0:T(8,128)(2,1)S(1)} all-to-all(bf16[8,256,256]{2,1,0:T(8,128)(2,1)} %bitcast.164), channel_id=1, replica_groups=mesh['dp'=8,'tensor'=4] {'dp'}, dimensions={0} | all-to-all | bytes 2097152 | tf_op jit(solution)/shard_map/all_to_all | solution.py:371
  155.4 45.1 %collective-permute-done.34 = bf16[512,2048]{1,0:T(8,128)(2,1)} collective-permute-done((bf16[512,2048]{1,0:T(8,128)(2,1)}, bf16[512,2048]{1,0:T(8,128)(2,1)}, u32[]{:S(2)}, u32[]{:S(2)}) %collective-permute-start.34) | collective-permute-done | bytes 2097184 | tf_op jit(solution)/shard_map/ppermute | solution.py:265
  213.5 7.3 all-to-all-done.1
  259.5 18.4 %collective-permute-done.14 = bf16[128,2048]{0,1:T(8,128)(2,1)S(1)} collective-permute-done((bf16[128,2048]{0,1:T(8,128)(2,1)S(1)}, bf16[128,2048]{0,1:T(8,128)(2,1)S(1)}, u32[]{:S(2)}, u32[]{:S(2)}) %collective-permute-start.14) | collective-permute-done | bytes 524320 | tf_op jit(solution)/shard_map/ppermute | solution.py:265
  287.1 17.6 %attend_forward.1 = (bf16[512,2048]{1,0:T(8,128)(2,1)}, f32[4,4,1,512]{3,2,1,0:T(1,128)}) custom-call(s32[3,4]{1,0:T(4,128)} %pad_add_fusion.info_ref, bf16[512,2304]{1,0:T(8,128)(2,1)} %copy-done.6, bf16[2048,256]{1,0:T(8,128)(2,1)} %all-gather.14.cloned.1.call-done.kv_ref, s32[1,512]{1,0:T(1,128)} %bitcast.180), custom_call_target="tpu_custom_call" | custom-call | tf_op jit(solution)/shard_map/attend_forward/pallas_call | solution.py:177
  304.7 7.8 fusion.46
  325.1 7.3 constant_dynamic-update-slice_fusion.33
  332.5 7.1 constant_dynamic-update-slice_fusion.15
  339.6 26.1 %collective-permute-done.21 = bf16[512,2048]{1,0:T(8,128)(2,1)} collective-permute-done((bf16[512,2048]{1,0:T(8,128)(2,1)}, bf16[512,2048]{1,0:T(8,128)(2,1)}, u32[]{:S(2)}, u32[]{:S(2)}) %collective-permute-start.21) | collective-permute-done | bytes 2097184 | tf_op jit(solution)/shard_map/ppermute | solution.py:265
  520.9 13.5 %collective-permute-done.30 = bf16[256,2048]{1,0:T(8,128)(2,1)S(1)} collective-permute-done((bf16[256,2048]{1,0:T(8,128)(2,1)S(1)}, bf16[256,2048]{1,0:T(8,128)(2,1)S(1)}, u32[]{:S(2)}, u32[]{:S(2)}) %collective-permute-start.30) | collective-permute-done | bytes 1048608 | tf_op jit(solution)/shard_map/ppermute | solution.py:265
  538.0 18.1 %collective-permute-done.46 = bf16[256,2048]{1,0:T(8,128)(2,1)S(1)} collective-permute-done((bf16[256,2048]{1,0:T(8,128)(2,1)S(1)}, bf16[256,2048]{1,0:T(8,128)(2,1)S(1)}, u32[]{:S(2)}, u32[]{:S(2)}) %collective-permute-start.46) | collective-permute-done | bytes 1048608 | tf_op jit(solution)/shard_map/ppermute | solution.py:265
  558.2 9.8 collective-permute-done.42
  580.8 67.5 %collective-permute-done.47 = bf16[512,2048]{1,0:T(8,128)(2,1)S(1)} collective-permute-done((bf16[512,2048]{1,0:T(8,128)(2,1)S(1)}, bf16[512,2048]{1,0:T(8,128)(2,1)S(1)}, u32[]{:S(2)}, u32[]{:S(2)}) %collective-permute-start.47) | collective-permute-done | bytes 2097184 | tf_op jit(solution)/shard_map/ppermute | solution.py:265
  652.0 10.4 collective-permute-done.27
  668.8 10.7 convolution_convert_fusion.10.grad_ref
  679.5 21.5 %attend_backward.1 = (bf16[512,2048]{1,0:T(8,128)(2,1)}, f32[2048,256]{1,0:T(8,128)}) custom-call(s32[3,4]{1,0:T(4,128)} %pad_add_fusion.info_ref, bf16[512,2304]{1,0:T(8,128)(2,1)} %copy-done.6, bf16[512,2048]{1,0:T(8,128)(2,1)} %convolution_convert_fusion.10.grad_ref, bf16[512,2048]{1,0:T(8,128)(2,1)} %get-tuple-element.20.o_ref, ...), custom_call_target="tpu_custom_call" | custom-call | tf_op jit(solution)/shard_map/attend_backward/pallas_call | solution.py:203
  704.4 23.8 %convolution_convert_fusion = bf16[1024,2048]{1,0:T(8,128)(2,1)} fusion(bf16[4096,1024]{1,0:T(8,128)(2,1)} %get-tuple-element.117, bf16[4096,2048]{1,0:T(8,128)(2,1)} %constant_dynamic-update-slice_fusion.34), kind=kOutput, calls=%fused_computation.40 | convolution fusion | flops 17181966336 | bytes 29360128 | tf_op jit(solution)/shard_map/dot_general | solution.py:21
  729.8 23.8 %convolution_convert_fusion.1 = bf16[1024,2048]{1,0:T(8,128)(2,1)} fusion(bf16[4096,1024]{1,0:T(8,128)(2,1)} %copy-done.10, bf16[4096,2048]{1,0:T(8,128)(2,1)} %constant_dynamic-update-slice_fusion.17), kind=kOutput, calls=%fused_computation.41 | convolution fusion | flops 17181966336 | bytes 29360128 | tf_op jit(solution)/shard_map/dot_general | solution.py:21
  806.5 57.0 %reduce-scatter.14.cloned.1.call-done = bf16[256,2048]{1,0:T(8,128)(2,1)} async-done(((bf16[1024,2048]{1,0:T(8,128)(2,1)}), bf16[256,2048]{1,0:T(8,128)(2,1)}) %reduce-scatter.14.cloned.1.call-update) | async-done | bytes 1048592 | tf_op jit(solution)/shard_map/reduce_scatter | solution.py:429
  865.8 77.3 %reduce-scatter.12.cloned.1.call-done = bf16[256,2048]{1,0:T(8,128)(2,1)} async-done(((bf16[1024,2048]{1,0:T(8,128)(2,1)}), bf16[256,2048]{1,0:T(8,128)(2,1)}) %reduce-scatter.12.cloned.1.call-update) | async-done | bytes 1048592 | tf_op jit(solution)/shard_map/reduce_scatter | solution.py:429
  974.5 12.1 %collective-permute-done.60 = bf16[256,2048]{0,1:T(8,128)(2,1)} collective-permute-done((bf16[256,2048]{0,1:T(8,128)(2,1)}, bf16[256,2048]{0,1:T(8,128)(2,1)}, u32[]{:S(2)}, u32[]{:S(2)}) %collective-permute-start.60) | collective-permute-done | bytes 1048608 | tf_op jit(solution)/shard_map/ppermute | solution.py:265
  1006.1 12.3 %collective-permute-done.51 = bf16[128,2304]{1,0:T(8,128)(2,1)S(1)} collective-permute-done((bf16[128,2304]{1,0:T(8,128)(2,1)S(1)}, bf16[128,2304]{1,0:T(8,128)(2,1)S(1)}, u32[]{:S(2)}, u32[]{:S(2)}) %collective-permute-start.51) | collective-permute-done | bytes 589856 | tf_op jit(solution)/shard_map/ppermute | solution.py:265
  1019.3 11.8 %fusion.14 = (f32[2048]{0:T(1024)}, f32[512]{0:T(512)}, f32[512]{0:T(512)}, f32[2048]{0:T(1024)}, f32[512,2048]{1,0:T(8,128)}) fusion(bf16[512,2048]{1,0:T(8,128)(2,1)S(1)} %copy-done.3, f32[512]{0:T(512)S(1)} %copy-done.45, f32[512]{0:T(512)S(1)} %copy-done.33, f32[2048]{0:T(1024)S(1)} %copy-done.41, ...), kind=kOutput, calls=%fused_computation.22 | convolution fusion | flops 4847037440 | bytes 18120704 | tf_op jit(solution)/shard_map/dot_general | solution.py:27
  1032.5 14.1 %collective-permute-done.52 = bf16[256,2304]{1,0:T(8,128)(2,1)S(1)} collective-permute-done((bf16[256,2304]{1,0:T(8,128)(2,1)S(1)}, bf16[256,2304]{1,0:T(8,128)(2,1)S(1)}, u32[]{:S(2)}, u32[]{:S(2)}) %collective-permute-start.52) | collective-permute-done | bytes 1179680 | tf_op jit(solution)/shard_map/ppermute | solution.py:265
  1053.3 16.4 %all-gather.6 = f32[4,1,15488]{2,1,0:T(1,128)S(1)} all-gather(f32[1,1,15488]{2,1,0:T(1,128)S(1)} %reshape.316), channel_id=4, replica_groups=mesh['dp'=8,'tensor'=4] {'tensor'}, dimensions={0}, use_global_device_ids=true | all-gather | bytes 309760 | tf_op jit(solution)/shard_map/all_gather | solution.py:483
  1072.9 8.7 all-gather.7
  1093.5 14.8 %reduce-scatter.8.cloned.1.call-done = bf16[1,256,512]{2,1,0:T(8,128)(2,1)} async-done(((bf16[4,256,512]{2,1,0:T(8,128)(2,1)}), bf16[1,256,512]{2,1,0:T(8,128)(2,1)}) %reduce-scatter.8.cloned.1.call-update) | async-done | bytes 262160 | tf_op jit(solution)/shard_map/reduce_scatter | solution.py:462
  (482 shorter events, 432.4 us)
Async XLA Ops:
  7.2 52.1 %all-gather.20.cloned.1.call-start = ((), (), s32[]{:S(2)}) async-start(), calls=%async_computation.17 | async-start | bytes 2621440 | tf_op jit(solution)/shard_map/all_gather | solution.py:352
  10.2 276.9 %all-gather.14.cloned.1.call-start = ((), (), s32[]{:S(2)}) async-start(), calls=%async_computation.9 | async-start | bytes 1310720 | tf_op jit(solution)/shard_map/all_gather | solution.py:385
  131.8 193.3 %all-gather.16.cloned.1.call-start = ((), (), s32[]{:S(2)}) async-start(), calls=%async_computation.10 | async-start | bytes 5242880 | tf_op jit(solution)/shard_map/all_gather | solution.py:372
  154.0 51.6 %collective-permute-start.37 = (bf16[512,2048]{1,0:T(8,128)(2,1)}, bf16[512,2048]{1,0:T(8,128)(2,1)}, u32[]{:S(2)}, u32[]{:S(2)}) collective-permute-start(bf16[512,2048]{1,0:T(8,128)(2,1)} %param.97), channel_id=1, source_target_pairs={{0,8},{4,12},{8,24},{12,28},{24,16},{28,20},{16,0},{20,4},{1,9},{5... | collective-permute-start | bytes 6291464 | tf_op jit(solution)/shard_map/ppermute | solution.py:265
  155.4 72.3 %collective-permute-start.32 = (bf16[512,2048]{1,0:T(8,128)(2,1)}, bf16[512,2048]{1,0:T(8,128)(2,1)}, u32[]{:S(2)}, u32[]{:S(2)}) collective-permute-start(bf16[512,2048]{1,0:T(8,128)(2,1)} %param.97), channel_id=1, source_target_pairs={{0,4},{4,0},{8,12},{12,8},{16,20},{20,16},{24,28},{28,24},{1,5},{5... | collective-permute-start | bytes 6291464 | tf_op jit(solution)/shard_map/ppermute | solution.py:265
  204.8 127.7 %all-gather.18.cloned.1.call-start = ((), (), s32[]{:S(2)}) async-start(), calls=%async_computation.11 | async-start | bytes 5242880 | tf_op jit(solution)/shard_map/all_gather | solution.py:372
  205.6 50.0 %collective-permute-start.44 = (bf16[512,2048]{1,0:T(8,128)(2,1)}, bf16[512,2048]{1,0:T(8,128)(2,1)}, u32[]{:S(2)}, u32[]{:S(2)}) collective-permute-start(bf16[512,2048]{1,0:T(8,128)(2,1)} %collective-permute-done.37), channel_id=1, source_target_pairs={{0,4},{4,0},{8,12},{12,8},{16,20},{20,16},{24,28},{28,24},{1,5},{5... | collective-permute-start | bytes 6291464 | tf_op jit(solution)/shard_map/ppermute | solution.py:265
  223.0 562.4 %reduce-scatter.6.cloned.1.call-start = ((), (), s32[]{:S(2)}) async-start(), calls=%async_computation.12 | async-start | bytes 2621440 | tf_op jit(solution)/shard_map/reduce_scatter | solution.py:445
  241.7 80.6 %collective-permute-start.39 = (bf16[256,2048]{1,0:T(8,128)(2,1)}, bf16[256,2048]{1,0:T(8,128)(2,1)}, u32[]{:S(2)}, u32[]{:S(2)}) collective-permute-start(bf16[256,2048]{1,0:T(8,128)(2,1)} %slice.248), channel_id=1, source_target_pairs={{8,0},{12,4},{24,8},{28,12},{16,24},{20,28},{0,16},{4,20},{9,1},{1... | collective-permute-start | bytes 3145736 | tf_op jit(solution)/shard_map/ppermute | solution.py:265
  255.6 65.1 %collective-permute-start.38 = (bf16[256,2048]{1,0:T(8,128)(2,1)}, bf16[256,2048]{1,0:T(8,128)(2,1)S(1)}, u32[]{:S(2)}, u32[]{:S(2)}) collective-permute-start(bf16[256,2048]{1,0:T(8,128)(2,1)} %slice.247), channel_id=1, source_target_pairs={{0,8},{4,12},{8,24},{12,28},{24,16},{28,20},{16,0},{20,4},{1,9},{5... | collective-permute-start | bytes 3145736 | tf_op jit(solution)/shard_map/ppermute | solution.py:265
  318.2 50.1 %collective-permute-start.18 = (bf16[512,2048]{1,0:T(8,128)(2,1)}, bf16[512,2048]{1,0:T(8,128)(2,1)}, u32[]{:S(2)}, u32[]{:S(2)}) collective-permute-start(bf16[512,2048]{1,0:T(8,128)(2,1)} %get-tuple-element.33), channel_id=1, source_target_pairs={{8,0},{12,4},{24,8},{28,12},{16,24},{20,28},{0,16},{4,20},{9,1},{1... | collective-permute-start | bytes 6291464 | tf_op jit(solution)/shard_map/ppermute | solution.py:265
  319.6 51.6 %collective-permute-start.16 = (bf16[512,2048]{1,0:T(8,128)(2,1)}, bf16[512,2048]{1,0:T(8,128)(2,1)}, u32[]{:S(2)}, u32[]{:S(2)}) collective-permute-start(bf16[512,2048]{1,0:T(8,128)(2,1)} %get-tuple-element.33), channel_id=1, source_target_pairs={{0,4},{4,0},{8,12},{12,8},{16,20},{20,16},{24,28},{28,24},{1,5},{5... | collective-permute-start | bytes 6291464 | tf_op jit(solution)/shard_map/ppermute | solution.py:265
  325.1 153.6 %collective-permute-start.40 = (bf16[512,2048]{1,0:T(8,128)(2,1)}, bf16[512,2048]{1,0:T(8,128)(2,1)}, u32[]{:S(2)}, u32[]{:S(2)}) collective-permute-start(bf16[512,2048]{1,0:T(8,128)(2,1)} %get-tuple-element.64), channel_id=1, source_target_pairs={{0,4},{4,0},{8,12},{12,8},{16,20},{20,16},{24,28},{28,24},{1,5},{5... | collective-permute-start | bytes 6291464 | tf_op jit(solution)/shard_map/ppermute | solution.py:265
  407.3 244.8 %collective-permute-start.17 = (bf16[512,2048]{1,0:T(8,128)(2,1)}, bf16[512,2048]{1,0:T(8,128)(2,1)}, u32[]{:S(2)}, u32[]{:S(2)}) collective-permute-start(bf16[512,2048]{1,0:T(8,128)(2,1)} %convolution_convert_fusion.9), channel_id=1, source_target_pairs={{0,4},{4,0},{8,12},{12,8},{16,20},{20,16},{24,28},{28,24},{1,5},{5... | collective-permute-start | bytes 6291464 | tf_op jit(solution)/shard_map/ppermute | solution.py:265
  412.1 160.2 %collective-permute-start.33 = (bf16[512,2048]{1,0:T(8,128)(2,1)}, bf16[512,2048]{1,0:T(8,128)(2,1)S(1)}, u32[]{:S(2)}, u32[]{:S(2)}) collective-permute-start(bf16[512,2048]{1,0:T(8,128)(2,1)} %convolution_convert_fusion.5), channel_id=1, source_target_pairs={{0,4},{4,0},{8,12},{12,8},{16,20},{20,16},{24,28},{28,24},{1,5},{5... | collective-permute-start | bytes 6291464 | tf_op jit(solution)/shard_map/ppermute | solution.py:265
  416.2 52.2 %collective-permute-start.24 = (bf16[512,2048]{1,0:T(8,128)(2,1)S(1)}, bf16[512,2048]{1,0:T(8,128)(2,1)S(1)}, u32[]{:S(2)}, u32[]{:S(2)}) collective-permute-start(bf16[512,2048]{1,0:T(8,128)(2,1)S(1)} %get-tuple-element.68), channel_id=1, source_target_pairs={{0,4},{4,0},{8,12},{12,8},{16,20},{20,16},{24,28},{28,24},{1,5},{5... | collective-permute-start | bytes 6291464 | tf_op jit(solution)/shard_map/ppermute | solution.py:265
  422.9 72.6 %collective-permute-start.20 = (bf16[512,2048]{1,0:T(8,128)(2,1)S(1)}, bf16[512,2048]{1,0:T(8,128)(2,1)S(1)}, u32[]{:S(2)}, u32[]{:S(2)}) collective-permute-start(bf16[512,2048]{1,0:T(8,128)(2,1)S(1)} %convolution_convert_fusion.8), channel_id=1, source_target_pairs={{0,4},{4,0},{8,12},{12,8},{16,20},{20,16},{24,28},{28,24},{1,5},{5... | collective-permute-start | bytes 6291464 | tf_op jit(solution)/shard_map/ppermute | solution.py:265
  520.9 50.3 %collective-permute-start.26 = (bf16[256,2048]{1,0:T(8,128)(2,1)S(1)}, bf16[256,2048]{1,0:T(8,128)(2,1)S(1)}, u32[]{:S(2)}, u32[]{:S(2)}) collective-permute-start(bf16[256,2048]{1,0:T(8,128)(2,1)S(1)} %get-tuple-element.55), channel_id=1, source_target_pairs={{0,8},{4,12},{8,24},{12,28},{24,16},{28,20},{16,0},{20,4},{1,9},{5... | collective-permute-start | bytes 3145736 | tf_op jit(solution)/shard_map/ppermute | solution.py:265
  556.1 95.9 %collective-permute-start.31 = (bf16[512,2048]{1,0:T(8,128)(2,1)}, bf16[512,2048]{1,0:T(8,128)(2,1)S(1)}, u32[]{:S(2)}, u32[]{:S(2)}) collective-permute-start(bf16[512,2048]{1,0:T(8,128)(2,1)} %pad_maximum_fusion.2), channel_id=1, source_target_pairs={{8,0},{12,4},{24,8},{28,12},{16,24},{20,28},{0,16},{4,20},{9,1},{1... | collective-permute-start | bytes 6291464 | tf_op jit(solution)/shard_map/ppermute | solution.py:265
  568.0 80.3 %collective-permute-start.47 = (bf16[512,2048]{1,0:T(8,128)(2,1)S(1)}, bf16[512,2048]{1,0:T(8,128)(2,1)S(1)}, u32[]{:S(2)}, u32[]{:S(2)}) collective-permute-start(bf16[512,2048]{1,0:T(8,128)(2,1)S(1)} %pad_maximum_fusion.4), channel_id=1, source_target_pairs={{8,0},{12,4},{24,8},{28,12},{16,24},{20,28},{0,16},{4,20},{9,1},{1... | collective-permute-start | bytes 6291464 | tf_op jit(solution)/shard_map/ppermute | solution.py:265
  571.1 77.2 %collective-permute-start.43 = (bf16[512,2048]{1,0:T(8,128)(2,1)}, bf16[512,2048]{1,0:T(8,128)(2,1)S(1)}, u32[]{:S(2)}, u32[]{:S(2)}) collective-permute-start(bf16[512,2048]{1,0:T(8,128)(2,1)} %pad_maximum_fusion.3), channel_id=1, source_target_pairs={{0,8},{4,12},{8,24},{12,28},{24,16},{28,20},{16,0},{20,4},{1,9},{5... | collective-permute-start | bytes 6291464 | tf_op jit(solution)/shard_map/ppermute | solution.py:265
  572.3 90.1 %collective-permute-start.27 = (bf16[512,2048]{1,0:T(8,128)(2,1)S(1)}, bf16[512,2048]{1,0:T(8,128)(2,1)S(1)}, u32[]{:S(2)}, u32[]{:S(2)}) collective-permute-start(bf16[512,2048]{1,0:T(8,128)(2,1)S(1)} %pad_maximum_fusion.1), channel_id=1, source_target_pairs={{0,8},{4,12},{8,24},{12,28},{24,16},{28,20},{16,0},{20,4},{1,9},{5... | collective-permute-start | bytes 6291464 | tf_op jit(solution)/shard_map/ppermute | solution.py:265
  701.0 162.5 %reduce-scatter.14.cloned.1.call-start = ((), (), s32[]{:S(2)}) async-start(), calls=%async_computation.16 | async-start | bytes 5242880 | tf_op jit(solution)/shard_map/reduce_scatter | solution.py:429
  728.3 214.9 %reduce-scatter.12.cloned.1.call-start = ((), (), s32[]{:S(2)}) async-start(), calls=%async_computation.15 | async-start | bytes 5242880 | tf_op jit(solution)/shard_map/reduce_scatter | solution.py:429
  769.9 204.6 %collective-permute-start.56 = (bf16[256,2048]{0,1:T(8,128)(2,1)}, bf16[256,2048]{0,1:T(8,128)(2,1)}, u32[]{:S(2)}, u32[]{:S(2)}) collective-permute-start(bf16[256,2048]{0,1:T(8,128)(2,1)} %get-tuple-element.44), channel_id=1, source_target_pairs={{0,4},{4,0},{8,12},{12,8},{16,20},{20,16},{24,28},{28,24},{1,5},{5... | collective-permute-start | bytes 3145736 | tf_op jit(solution)/shard_map/ppermute | solution.py:265
  796.0 153.1 %collective-permute-start.53 = (bf16[256,2304]{1,0:T(8,128)(2,1)}, bf16[256,2304]{1,0:T(8,128)(2,1)}, u32[]{:S(2)}, u32[]{:S(2)}) collective-permute-start(bf16[256,2304]{1,0:T(8,128)(2,1)} %get-tuple-element.38), channel_id=1, source_target_pairs={{0,4},{4,0},{8,12},{12,8},{16,20},{20,16},{24,28},{28,24},{1,5},{5... | collective-permute-start | bytes 3538952 | tf_op jit(solution)/shard_map/ppermute | solution.py:265
  796.0 155.1 %collective-permute-start.50 = (bf16[256,2304]{1,0:T(8,128)(2,1)}, bf16[256,2304]{1,0:T(8,128)(2,1)}, u32[]{:S(2)}, u32[]{:S(2)}) collective-permute-start(bf16[256,2304]{1,0:T(8,128)(2,1)} %get-tuple-element.39), channel_id=1, source_target_pairs={{0,4},{4,0},{8,12},{12,8},{16,20},{20,16},{24,28},{28,24},{1,5},{5... | collective-permute-start | bytes 3538952 | tf_op jit(solution)/shard_map/ppermute | solution.py:265
  798.7 152.4 %collective-permute-start.49 = (bf16[256,2304]{1,0:T(8,128)(2,1)}, bf16[256,2304]{1,0:T(8,128)(2,1)}, u32[]{:S(2)}, u32[]{:S(2)}) collective-permute-start(bf16[256,2304]{1,0:T(8,128)(2,1)} %get-tuple-element.40), channel_id=1, source_target_pairs={{0,4},{4,0},{8,12},{12,8},{16,20},{20,16},{24,28},{28,24},{1,5},{5... | collective-permute-start | bytes 3538952 | tf_op jit(solution)/shard_map/ppermute | solution.py:265
  802.8 171.7 %collective-permute-start.63 = (bf16[256,2048]{0,1:T(8,128)(2,1)}, bf16[256,2048]{0,1:T(8,128)(2,1)}, u32[]{:S(2)}, u32[]{:S(2)}) collective-permute-start(bf16[256,2048]{0,1:T(8,128)(2,1)} %pad_maximum_fusion.9), channel_id=1, source_target_pairs={{8,0},{12,4},{24,8},{28,12},{16,24},{20,28},{0,16},{4,20},{9,1},{1... | collective-permute-start | bytes 3145736 | tf_op jit(solution)/shard_map/ppermute | solution.py:265
  969.2 120.5 %reduce-scatter.10.cloned.1.call-start = ((), (), s32[]{:S(2)}) async-start(), calls=%async_computation.14 | async-start | bytes 1310720 | tf_op jit(solution)/shard_map/reduce_scatter | solution.py:462
  990.6 100.9 %all-gather.22.cloned.1.call-start = ((), (), s32[]{:S(2)}) async-start(), calls=%async_computation.18 | async-start | bytes 1310720 | tf_op jit(solution)/shard_map/all_gather | solution.py:467
  1051.0 57.3 %reduce-scatter.8.cloned.1.call-start = ((), (), s32[]{:S(2)}) async-start(), calls=%async_computation.13 | async-start | bytes 1310720 | tf_op jit(solution)/shard_map/reduce_scatter | solution.py:462
  (117 other events, 2275.5 us)
Sparse Core Ops, SparseCore 0:
  10.3 48.9 all-gather.19
  132.0 25.9 all-gather.13
  160.1 80.0 all-gather.15
  242.2 78.7 all-gather.17
  701.1 83.9 reduce-scatter.5
  787.4 76.1 reduce-scatter.13
  865.8 77.2 reduce-scatter.11
  990.7 26.8 reduce-scatter.9
  1051.1 29.1 all-gather.21
  1082.5 25.7 reduce-scatter.7
